TPU v7x, 32 devices: a whole 2x2x4 slice. The times are simulated.
32 devices in a mesh: ctx: 8 (over z, y), grp: 4 (over x, core).
Axes of the slice: x: 2, y: 2, z: 4, core: 2. Of those that a mesh axis runs over, the one named last changes fastest.
Arguments:
- streams: bfloat16 [3, 3072, 4096], P(None, 'ctx', 'grp'), may hold values from -400 to 400
- filters: bfloat16 [3, 256, 128], P(None, 'grp'), may hold values from -0.5 to 0.5
- gain: float32 [4096], P('grp'), may hold values from 0.5 to 1.5
Outputs:
- normed: bfloat16 [3072, 4096], P('ctx', 'grp')
All inputs are finite; a program needn't handle non-finite values.
Results may differ from a plain program's by a relative error of at most 0.012.
The roundings to bfloat16 on the way count: a program that leaves them out, or rounds other values in their place, can miss the bound.
Values may be sent and summed in bfloat16 or wider, within the bound.
A program may use at most 128 MiB of HBM per device.

v0:
```python
import math
import jax
import jax.numpy as jnp
import numpy as np
from jax import lax
from jax.sharding import PartitionSpec as P

HD = 128
CH = 4096


def passed_along(block, axis, distance):
    devices = range(lax.axis_size(axis))
    route = [(i - distance, i) for i in devices if i - distance in devices]
    return lax.ppermute(block, axis, route)


def filter_all(streams, filters):
    tok_rows = streams.shape[1]
    chan_count = streams.shape[2]
    filt_len = filters.shape[2]
    group_count = filters.shape[1]
    group_width = chan_count // group_count
    tail = streams[:, tok_rows - filt_len :, :]
    before = passed_along(tail, "ctx", 1)
    padded = jnp.concatenate([before, streams], axis=1)
    block_count = tok_rows // filt_len
    blocks = padded.reshape(3, block_count + 1, filt_len, group_count, group_width)
    lag_table = np.arange(filt_len)[:, None] - np.arange(filt_len)[None, :]
    lower_idx = np.where(lag_table >= 0, lag_table, 0)
    upper_idx = np.where(lag_table < 0, lag_table + filt_len, 0)
    lower = jnp.where(lag_table >= 0, filters[:, :, lower_idx], 0.0)
    upper = jnp.where(lag_table < 0, filters[:, :, upper_idx], 0.0)
    result = jnp.einsum(
        "agts,absgc->abtgc", lower, blocks[:, 1:], preferred_element_type=jnp.float32
    )
    result = result + jnp.einsum(
        "agts,absgc->abtgc", upper, blocks[:, :-1], preferred_element_type=jnp.float32
    )
    return result.reshape(3, tok_rows, chan_count).astype(jnp.bfloat16)


def attend(queries, positions, keyed, valued):
    tok_rows, chan_count = queries.shape
    head_count = chan_count // HD
    scale = HD ** (-0.5)
    query_heads = queries.reshape(tok_rows, head_count, HD)
    query_last = jnp.max(positions)
    start_state = (
        jnp.full((head_count, tok_rows), -1e30, jnp.float32),
        jnp.zeros((head_count, tok_rows), jnp.float32),
        jnp.zeros((tok_rows, head_count, HD), jnp.float32),
    )
    key_piece = lax.all_gather(keyed, "ctx", axis=0, tiled=True)
    value_piece = lax.all_gather(valued, "ctx", axis=0, tiled=True)
    piece_len = key_piece.shape[0]
    block_len = math.gcd(piece_len, 512)

    def step_block(step_idx, state):
        offset = step_idx * block_len
        key_block = lax.dynamic_slice_in_dim(key_piece, offset, block_len, 0).reshape(
            block_len, head_count, HD
        )
        value_block = lax.dynamic_slice_in_dim(value_piece, offset, block_len, 0).reshape(
            block_len, head_count, HD
        )
        key_pos = offset + jnp.arange(block_len, dtype=jnp.int32)

        def update_block(inner):
            running, totals, accum = inner
            scores = (
                jnp.einsum(
                    "shd,khd->hsk", query_heads, key_block, preferred_element_type=jnp.float32
                )
                * scale
            )
            causal = key_pos[None, None, :] <= positions[None, :, None]
            newtop = jnp.maximum(running, jnp.max(jnp.where(causal, scores, -1e30), axis=2))
            weights = jnp.where(causal, jnp.exp(scores - newtop[:, :, None]), 0.0)
            factor = jnp.exp(running - newtop)
            totals = totals * factor + jnp.sum(weights, axis=2)
            accum = accum * factor.T[:, :, None] + jnp.einsum(
                "hsk,khd->shd",
                weights.astype(jnp.bfloat16),
                value_block,
                preferred_element_type=jnp.float32,
            )
            return (newtop, totals, accum)

        return lax.cond(offset > query_last, lambda inner: inner, update_block, state)

    running, totals, accum = lax.fori_loop(0, piece_len // block_len, step_block, start_state)
    return (accum / totals.T[:, :, None]).reshape(tok_rows, chan_count).astype(jnp.bfloat16)


def local(streams, filters, gain):
    features = filter_all(streams, filters)
    tok_rows = streams.shape[1]
    my_index = lax.axis_index("ctx")
    queries = features[0]
    positions = my_index * tok_rows + jnp.arange(tok_rows, dtype=jnp.int32)
    attended = attend(queries, positions, features[1], features[2])
    wide = attended.astype(jnp.float32)
    power = lax.psum(jnp.sum(wide * wide, axis=1), "grp") / CH
    return (wide * gain[None, :] * lax.rsqrt(power + 1e-06)[:, None]).astype(jnp.bfloat16)


def solution(mesh):
    placed = (P(None, "ctx", "grp"), P(None, "grp", None), P("grp"))
    return jax.shard_map(
        local, mesh=mesh, in_specs=placed, out_specs=P("ctx", "grp"), check_vma=False
    )
```

profile of v0, /device:TPU:24, one launch (start us, length us, event | category | flops | bytes accessed | tf_op | source)
XLA Modules:
  0.0 568.2 jit_solution(7154377040794997620)
XLA Ops:
  6.5 1.2 slice.21
  7.7 3.4 collective-permute-start
  13.0 112.9 %gather_fusion.1 = bf16[16384,3,64]{2,1,0:T(4,128)(2,1)} fusion(bf16[3,64,128]{1,0,2:T(4,128)(2,1)S(1)} %copy.17, s32[16384]{0:T(1024)S(1)} %broadcast_clamp_fusion), kind=kCustom, calls=%fused_computation.1 | custom fusion | bytes 12648448 | tf_op jit(solution)/shard_map/gather | solution.py:33
  125.9 17.2 %copy.21 = bf16[128,128,3,64]{1,0,3,2:T(8,128)(2,1)} copy(bf16[128,128,3,64]{3,2,1,0:T(4,128)(2,1)} %bitcast.81) | data formatting | bytes 12582912 | tf_op jit(solution)/shard_map/gather | solution.py:33
  143.1 112.7 %gather_fusion = bf16[16384,3,64]{2,1,0:T(4,128)(2,1)} fusion(bf16[3,64,128]{1,0,2:T(4,128)(2,1)S(1)} %copy.17, s32[16384]{0:T(1024)S(1)} %broadcast_clamp_fusion.1), kind=kCustom, calls=%fused_computation | custom fusion | bytes 12648448 | tf_op jit(solution)/shard_map/gather | solution.py:32
  255.9 17.2 %copy.18 = bf16[128,128,3,64]{1,0,3,2:T(8,128)(2,1)} copy(bf16[128,128,3,64]{3,2,1,0:T(4,128)(2,1)} %bitcast.80) | data formatting | bytes 12582912 | tf_op jit(solution)/shard_map/gather | solution.py:32
  273.1 2.1 pad_maximum_fusion
  275.2 3.0 copy.15
  278.2 5.7 %reshape.74 = bf16[3,4,128,64,16]{2,1,4,3,0:T(4,128)(2,1)} reshape(bf16[3,512,1024]{1,2,0:T(8,128)(2,1)} %copy.15) | data formatting | bytes 6291456 | tf_op jit(solution)/shard_map/reshape | solution.py:28
  283.9 8.0 %fusion.40 = (bf16[3,3,128,64,16]{2,1,4,3,0:T(4,128)(2,1)}, bf16[3,3,128,64,16]{2,1,4,3,0:T(4,128)(2,1)S(1)}) fusion(bf16[3,4,128,64,16]{2,1,4,3,0:T(4,128)(2,1)} %reshape.74), kind=kLoop, calls=%fused_computation.56 | loop fusion | bytes 9437184 | tf_op jit(solution)/shard_map/slice | solution.py:35
  292.0 6.0 %fusion.18 = f32[3,64,3,16,128]{4,3,2,1,0:T(8,128)} fusion(bf16[128,128,3,64]{1,0,3,2:T(8,128)(2,1)S(1)} %bitcast.79, pred[128,128]{1,0:T(8,128)(4,1)S(1)} %bitcast.89, bf16[3,3,128,64,16]{2,1,4,3,0:T(4,128)(2,1)S(1)} %get-tuple-element.351), kind=kOutput, calls=%fused_computation.26 | convolution fusion | flops 305135616 | bytes 13385728 | tf_op jit(solution)/shard_map/agts,absgc->abtgc/dot_general | solution.py:37
  298.1 7.8 %fusion.28 = bf16[3,3,128,64,16]{2,4,1,3,0:T(8,128)(2,1)S(1)} fusion(f32[3,64,3,16,128]{4,3,2,1,0:T(8,128)} %fusion.18, bf16[128,128,3,64]{1,0,3,2:T(8,128)(2,1)S(1)} %bitcast.77, pred[128,128]{1,0:T(8,128)(4,1)S(1)} %bitcast.88, bf16[3,3,128,64,16]{2,1,4,3,0:T(4,128)(2,1)} %get-tuple-element.350), kind=kOutput, calls=%fused_computation.38 | convolution fusion | flops 307494912 | bytes 15745024 | tf_op jit(solution)/shard_map/agts,absgc->abtgc/dot_general | solution.py:34
  308.6 1.1 copy.46
  312.0 93.6 %all-gather.3.cloned.1.call-done = bf16[3072,1024]{0,1:T(8,128)(2,1)} async-done(((bf16[384,1024]{0,1:T(8,128)(2,1)}), bf16[3072,1024]{0,1:T(8,128)(2,1)}) %all-gather.3.cloned.1.call-update) | async-done | bytes 6291472 | tf_op jit(solution)/shard_map/all_gather | solution.py:54
  405.6 99.8 %all-gather.5.cloned.1.call-done = bf16[3072,1024]{0,1:T(8,128)(2,1)} async-done(((bf16[384,1024]{0,1:T(8,128)(2,1)}), bf16[3072,1024]{0,1:T(8,128)(2,1)}) %all-gather.5.cloned.1.call-update) | async-done | bytes 6291472 | tf_op jit(solution)/shard_map/all_gather | solution.py:55
  505.5 47.3 %while.18 = (s32[]{:T(128)}, f32[8,384]{1,0:T(8,128)S(1)}, f32[8,384]{1,0:T(8,128)S(1)}, f32[384,8,128]{2,0,1:T(8,128)S(1)}, s32[]{:T(128)}, /*index=5*/bf16[307...) while((s32[]{:T(128)}, f32[8,384]{1,0:T(8,128)S(1)}, ...), condition=%wide.region_6.7_spmd.clone, body=%wide.region_1.6_spmd.clone.sunk | while | flops 823601024 | bytes 30095668 | solution.py:92
  506.2 7.3 %conditional.3 = (f32[8,384]{1,0:T(8,128)S(1)}, f32[8,384]{1,0:T(8,128)S(1)}, f32[384,8,128]{2,0,1:T(8,128)S(1)}) conditional(s32[]{:T(128)} %convert_element_type.65, (s32[]{:T(128)}, s32[512]{0:T(512)S(1)}, s32[]{:T(128)}, bf16[3072,1024]{0,1:T(8,128)(2,1)}, bf16[384,8,128]{2,0,1:T(8,128)(2,1)S(1)}, /*index=5*/f32[8,384]{1,0:T(8,128)S(1)}, ...), branch_computations={%region_2.4_spmd, %region_5.5_spmd} | conditional | flops 823601024 | bytes 30067270 | solution.py:90
  506.2 1.7 constant_dynamic-slice_fusion
  508.1 1.5 fusion.2
  509.6 2.5 bitcast_add_fusion
  512.1 1.3 fusion.6
  514.0 7.3 %conditional.3 = (f32[8,384]{1,0:T(8,128)S(1)}, f32[8,384]{1,0:T(8,128)S(1)}, f32[384,8,128]{2,0,1:T(8,128)S(1)}) conditional(s32[]{:T(128)} %convert_element_type.65, (s32[]{:T(128)}, s32[512]{0:T(512)S(1)}, s32[]{:T(128)}, bf16[3072,1024]{0,1:T(8,128)(2,1)}, bf16[384,8,128]{2,0,1:T(8,128)(2,1)S(1)}, /*index=5*/f32[8,384]{1,0:T(8,128)S(1)}, ...), branch_computations={%region_2.4_spmd, %region_5.5_spmd} | conditional | flops 823601024 | bytes 30067270 | solution.py:90
  514.1 1.7 constant_dynamic-slice_fusion
  516.0 1.5 fusion.2
  517.5 2.5 bitcast_add_fusion
  520.0 1.3 fusion.6
  521.9 7.3 %conditional.3 = (f32[8,384]{1,0:T(8,128)S(1)}, f32[8,384]{1,0:T(8,128)S(1)}, f32[384,8,128]{2,0,1:T(8,128)S(1)}) conditional(s32[]{:T(128)} %convert_element_type.65, (s32[]{:T(128)}, s32[512]{0:T(512)S(1)}, s32[]{:T(128)}, bf16[3072,1024]{0,1:T(8,128)(2,1)}, bf16[384,8,128]{2,0,1:T(8,128)(2,1)S(1)}, /*index=5*/f32[8,384]{1,0:T(8,128)S(1)}, ...), branch_computations={%region_2.4_spmd, %region_5.5_spmd} | conditional | flops 823601024 | bytes 30067270 | solution.py:90
  521.9 1.7 constant_dynamic-slice_fusion
  523.8 1.5 fusion.2
  525.4 2.5 bitcast_add_fusion
  527.8 1.3 fusion.6
  529.8 7.3 %conditional.3 = (f32[8,384]{1,0:T(8,128)S(1)}, f32[8,384]{1,0:T(8,128)S(1)}, f32[384,8,128]{2,0,1:T(8,128)S(1)}) conditional(s32[]{:T(128)} %convert_element_type.65, (s32[]{:T(128)}, s32[512]{0:T(512)S(1)}, s32[]{:T(128)}, bf16[3072,1024]{0,1:T(8,128)(2,1)}, bf16[384,8,128]{2,0,1:T(8,128)(2,1)S(1)}, /*index=5*/f32[8,384]{1,0:T(8,128)S(1)}, ...), branch_computations={%region_2.4_spmd, %region_5.5_spmd} | conditional | flops 823601024 | bytes 30067270 | solution.py:90
  529.8 1.7 constant_dynamic-slice_fusion
  531.7 1.5 fusion.2
  533.2 2.5 bitcast_add_fusion
  535.7 1.3 fusion.6
  537.7 7.3 %conditional.3 = (f32[8,384]{1,0:T(8,128)S(1)}, f32[8,384]{1,0:T(8,128)S(1)}, f32[384,8,128]{2,0,1:T(8,128)S(1)}) conditional(s32[]{:T(128)} %convert_element_type.65, (s32[]{:T(128)}, s32[512]{0:T(512)S(1)}, s32[]{:T(128)}, bf16[3072,1024]{0,1:T(8,128)(2,1)}, bf16[384,8,128]{2,0,1:T(8,128)(2,1)S(1)}, /*index=5*/f32[8,384]{1,0:T(8,128)S(1)}, ...), branch_computations={%region_2.4_spmd, %region_5.5_spmd} | conditional | flops 823601024 | bytes 30067270 | solution.py:90
  537.7 1.7 constant_dynamic-slice_fusion
  539.6 1.5 fusion.2
  541.1 2.5 bitcast_add_fusion
  543.6 1.3 fusion.6
  545.6 7.3 %conditional.3 = (f32[8,384]{1,0:T(8,128)S(1)}, f32[8,384]{1,0:T(8,128)S(1)}, f32[384,8,128]{2,0,1:T(8,128)S(1)}) conditional(s32[]{:T(128)} %convert_element_type.65, (s32[]{:T(128)}, s32[512]{0:T(512)S(1)}, s32[]{:T(128)}, bf16[3072,1024]{0,1:T(8,128)(2,1)}, bf16[384,8,128]{2,0,1:T(8,128)(2,1)S(1)}, /*index=5*/f32[8,384]{1,0:T(8,128)S(1)}, ...), branch_computations={%region_2.4_spmd, %region_5.5_spmd} | conditional | flops 823601024 | bytes 30067270 | solution.py:90
  545.6 1.7 constant_dynamic-slice_fusion
  547.5 1.5 fusion.2
  549.0 2.5 bitcast_add_fusion
  551.5 1.3 fusion.6
  553.4 6.8 %psum.7 = f32[384]{0:T(512)S(1)} all-reduce(f32[384]{0:T(512)S(1)} %get-tuple-element.344), channel_id=1, replica_groups=mesh['ctx'=8,'grp'=4] {'grp'}, use_global_device_ids=true, to_apply=%region_8.9 | all-reduce | flops 384 | bytes 3072 | tf_op jit(solution)/shard_map/psum | solution.py:104
  560.3 1.1 fusion.37
  (87 shorter events, 8.8 us)
Async XLA Ops:
  6.5 399.1 %all-gather.3.cloned.1.call-start = ((), (), s32[]{:S(2)}) async-start(), calls=%async_computation | async-start | bytes 7077888 | tf_op jit(solution)/shard_map/all_gather | solution.py:54
  7.7 265.4 %collective-permute-start = (bf16[3,128,1024]{2,1,0:T(8,128)(2,1)S(1)}, bf16[3,128,1024]{2,1,0:T(8,128)(2,1)}, u32[]{:S(2)}, u32[]{:S(2)}) collective-permute-start(bf16[3,128,1024]{2,1,0:T(8,128)(2,1)S(1)} %slice.21), channel_id=1, source_target_pairs={{0,4},{4,8},{8,12},{12,16},{16,20},{20,24},{24,28},{1,5},{5,9},{9,... | collective-permute-start | bytes 2359304 | tf_op jit(solution)/shard_map/ppermute | solution.py:15
  125.9 17.3 %copy-start.2 = (s32[16384]{0:T(1024)S(1)}, s32[16384]{0:T(1024)}, u32[]{:S(2)}) copy-start(s32[16384]{0:T(1024)} %constant.103) | copy-start | bytes 196612
  278.2 13.7 %slice-start.2 = ((s8[6291456]{0:T(1024)(128)(4,1)}), s8[2097152]{0:T(1024)(128)(4,1)S(1)}, s32[]{:S(2)}) async-start(s8[6291456]{0:T(1024)(128)(4,1)} %bitcast.78), calls=%async_computation.4 | async-start | bytes 4194304
  283.9 8.1 %slice-start.3 = ((s8[6291456]{0:T(1024)(128)(4,1)}), s8[4194304]{0:T(1024)(128)(4,1)S(1)}, s32[]{:S(2)}) async-start(s8[6291456]{0:T(1024)(128)(4,1)} %bitcast.78), calls=%async_computation.5 | async-start | bytes 8388608
  283.9 8.1 %copy-start.1 = (pred[128,128]{1,0:T(32,128)(4,1)S(1)}, pred[128,128]{1,0:T(32,128)(4,1)}, u32[]{:S(2)}) copy-start(pred[128,128]{1,0:T(32,128)(4,1)} %constant.100.clone) | copy-start | bytes 49156
  283.9 14.1 %slice-start = ((s8[6291456]{0:T(1024)(128)(4,1)}), s8[4194304]{0:T(1024)(128)(4,1)S(1)}, s32[]{:S(2)}) async-start(s8[6291456]{0:T(1024)(128)(4,1)} %bitcast.76), calls=%async_computation.2 | async-start | bytes 8388608
  292.0 6.1 %slice-start.1 = ((s8[6291456]{0:T(1024)(128)(4,1)}), s8[2097152]{0:T(1024)(128)(4,1)S(1)}, s32[]{:S(2)}) async-start(s8[6291456]{0:T(1024)(128)(4,1)} %bitcast.76), calls=%async_computation.3 | async-start | bytes 4194304
  292.0 6.1 %copy-start = (pred[128,128]{1,0:T(32,128)(4,1)S(1)}, pred[128,128]{1,0:T(32,128)(4,1)}, u32[]{:S(2)}) copy-start(pred[128,128]{1,0:T(32,128)(4,1)} %constant.98.clone) | copy-start | bytes 49156
  307.9 197.5 %all-gather.5.cloned.1.call-start = ((), (), s32[]{:S(2)}) async-start(), calls=%async_computation.1 | async-start | bytes 7077888 | tf_op jit(solution)/shard_map/all_gather | solution.py:55
  505.5 54.7 %copy-start.3 = (f32[1024]{0:T(1024)S(1)}, f32[1024]{0:T(1024)}, u32[]{:S(2)}) copy-start(f32[1024]{0:T(1024)} %param.15) | copy-start | bytes 12292
Sparse Core Ops, SparseCore 0:
  308.0 97.6 all-gather.2
  407.7 97.6 all-gather.4
where the time goes:
time: 570 us; the launch traced here: 568 us
  local copies, waits for them, and re-layouts  294 us (52%)
  waiting for transfers between devices  193 us (34%)
  matrix products  37.7 us (7%)
  other arithmetic  14.4 us (3%)
  between operations  13.6 us (2%)
  blocking collectives  6.84 us (1%)
    gather x2, local copies, waits for them, and re-layouts, filter_all(): upper = jnp.where(lag_table < 0, filters[:, :, upper_idx], 0.0)  130 us
    gather x2, local copies, waits for them, and re-layouts, filter_all(): lower = jnp.where(lag_table >= 0, filters[:, :, lower_idx], 0.0)  130 us
    all_gather x1, waiting for transfers between devices, attend(): value_piece = lax.all_gather(valued, 'ctx', axis=0, tiled=True)  99.8 us
    all_gather x1, waiting for transfers between devices, attend(): key_piece = lax.all_gather(keyed, 'ctx', axis=0, tiled=True)  93.6 us
    dot_general x6, matrix products, update_block(): jnp.einsum('hsk,khd->shd', weights.astype(jnp.bfloat16), value_block, pre...  14.9 us
  transfers between devices with their start and end apart: 3, of which 2 were waited for; matrix products, arithmetic and copies ran while one was open for 47% of the time, Pallas kernels for 0%

commit v1 on v0

--- a/solution.py
+++ b/solution.py
@@ -52,7 +52,12 @@
         jnp.zeros((tok_rows, head_count, HD), jnp.float32),
     )
     key_piece = lax.all_gather(keyed, "ctx", axis=0, tiled=True)
-    value_piece = lax.all_gather(valued, "ctx", axis=0, tiled=True)
+    ring = [valued]
+    for hop in range(7):
+        ring.append(lax.ppermute(ring[-1], "ctx", [(dev, (dev + 1) % 8) for dev in range(8)]))
+    value_piece = jnp.roll(
+        jnp.concatenate(ring[::-1], axis=0), (lax.axis_index("ctx") + 1) * ring[0].shape[0], axis=0
+    )
     piece_len = key_piece.shape[0]
     block_len = math.gcd(piece_len, 512)
 

time: 570 us -> 601 us (1.054)
  local copies, waits for them, and re-layouts: 294 us -> 317 us
  waiting for transfers between devices: 193 us -> 203 us
    ppermute x0 -> x7, waiting for transfers between devices: none -> 203 us  [attend(): lax.ppermute(ring[-1], 'ctx', [(dev, (dev + 1) % 8) for dev in range(8)])]
    all_gather x1 -> x0, waiting for transfers between devices: 99.8 us -> none  [attend(): value_piece = lax.all_gather(valued, 'ctx', axis=0, tiled=True)]
    all_gather x1, waiting for transfers between devices: 93.6 us -> 0.01 us  [attend(): key_piece = lax.all_gather(keyed, 'ctx', axis=0, tiled=True)]
    unnamed x20 -> x55, local copies, waits for them, and re-layouts: 3.46 us -> 19.6 us
    dynamic_slice x0 -> x1, local copies, waits for them, and re-layouts: none -> 6.15 us  [attend(): jnp.roll(jnp.concatenate(ring[::-1], axis=0), (lax.axis_index('ctx') + 1)...]
  transfers between devices with their start and end apart: 3 -> 9, of which waited for: 2 -> 7; matrix products, arithmetic and copies ran while one was open for 47% -> 47% of each run, Pallas kernels for 0% -> 0%
where the time goes in v1:
time: 601 us; the launch traced here: 599 us
  local copies, waits for them, and re-layouts  317 us (53%)
  waiting for transfers between devices  203 us (34%)
  matrix products  37.7 us (6%)
  other arithmetic  14.4 us (2%)
  between operations  13.8 us (2%)
    ppermute x7, waiting for transfers between devices, attend(): lax.ppermute(ring[-1], 'ctx', [(dev, (dev + 1) % 8) for dev in range(8)])  203 us
    gather x2, local copies, waits for them, and re-layouts, filter_all(): upper = jnp.where(lag_table < 0, filters[:, :, upper_idx], 0.0)  130 us
    gather x2, local copies, waits for them, and re-layouts, filter_all(): lower = jnp.where(lag_table >= 0, filters[:, :, lower_idx], 0.0)  130 us
    unnamed x55, local copies, waits for them, and re-layouts  19.6 us
    dot_general x6, matrix products, update_block(): jnp.einsum('hsk,khd->shd', weights.astype(jnp.bfloat16), value_block, pre...  14.9 us
  transfers between devices with their start and end apart: 9, of which 7 were waited for; matrix products, arithmetic and copies ran while one was open for 47% of the time, Pallas kernels for 0%

profile of v1, /device:TPU:24, one launch (start us, length us, event | category | flops | bytes accessed | tf_op | source)
XLA Modules:
  0.0 599.4 jit_solution(17689433364415602130)
XLA Ops:
  7.7 3.4 collective-permute-start
  13.0 112.7 %gather_fusion.1 = bf16[16384,3,64]{2,1,0:T(4,128)(2,1)} fusion(bf16[3,64,128]{1,0,2:T(4,128)(2,1)S(1)} %copy.17, s32[16384]{0:T(1024)S(1)} %broadcast_clamp_fusion), kind=kCustom, calls=%fused_computation.1 | custom fusion | bytes 12648448 | tf_op jit(solution)/shard_map/gather | solution.py:33
  125.7 17.2 %copy.21 = bf16[128,128,3,64]{1,0,3,2:T(8,128)(2,1)} copy(bf16[128,128,3,64]{3,2,1,0:T(4,128)(2,1)} %bitcast.85) | data formatting | bytes 12582912 | tf_op jit(solution)/shard_map/gather | solution.py:33
  143.0 112.6 %gather_fusion = bf16[16384,3,64]{2,1,0:T(4,128)(2,1)} fusion(bf16[3,64,128]{1,0,2:T(4,128)(2,1)S(1)} %copy.17, s32[16384]{0:T(1024)S(1)} %broadcast_clamp_fusion.1), kind=kCustom, calls=%fused_computation | custom fusion | bytes 12648448 | tf_op jit(solution)/shard_map/gather | solution.py:32
  255.5 17.2 %copy.18 = bf16[128,128,3,64]{1,0,3,2:T(8,128)(2,1)} copy(bf16[128,128,3,64]{3,2,1,0:T(4,128)(2,1)} %bitcast.84) | data formatting | bytes 12582912 | tf_op jit(solution)/shard_map/gather | solution.py:32
  272.7 2.1 pad_maximum_fusion
  274.9 3.0 copy.15
  277.8 5.6 reshape.74
  283.5 8.1 %fusion.40 = (bf16[3,3,128,64,16]{2,1,4,3,0:T(4,128)(2,1)}, bf16[3,3,128,64,16]{2,1,4,3,0:T(4,128)(2,1)S(1)}) fusion(bf16[3,4,128,64,16]{2,1,4,3,0:T(4,128)(2,1)} %reshape.74), kind=kLoop, calls=%fused_computation.73 | loop fusion | bytes 9437184 | tf_op jit(solution)/shard_map/slice | solution.py:35
  291.6 6.0 %fusion.18 = f32[3,64,3,16,128]{4,3,2,1,0:T(8,128)} fusion(bf16[128,128,3,64]{1,0,3,2:T(8,128)(2,1)S(1)} %bitcast.83, pred[128,128]{1,0:T(8,128)(4,1)S(1)} %bitcast.95, bf16[3,3,128,64,16]{2,1,4,3,0:T(4,128)(2,1)S(1)} %get-tuple-element.351), kind=kOutput, calls=%fused_computation.26 | convolution fusion | flops 305135616 | bytes 13385728 | tf_op jit(solution)/shard_map/agts,absgc->abtgc/dot_general | solution.py:37
  297.7 7.8 %fusion.28 = bf16[3,3,128,64,16]{2,4,1,3,0:T(8,128)(2,1)S(1)} fusion(f32[3,64,3,16,128]{4,3,2,1,0:T(8,128)} %fusion.18, bf16[128,128,3,64]{1,0,3,2:T(8,128)(2,1)S(1)} %bitcast.81, pred[128,128]{1,0:T(8,128)(4,1)S(1)} %bitcast.94, bf16[3,3,128,64,16]{2,1,4,3,0:T(4,128)(2,1)} %get-tuple-element.350), kind=kOutput, calls=%fused_computation.38 | convolution fusion | flops 307494912 | bytes 15745024 | tf_op jit(solution)/shard_map/agts,absgc->abtgc/dot_general | solution.py:34
  308.2 28.3 %collective-permute-done.1 = bf16[384,1024]{0,1:T(8,128)(2,1)S(1)} collective-permute-done((bf16[384,1024]{0,1:T(8,128)(2,1)S(1)}, bf16[384,1024]{0,1:T(8,128)(2,1)S(1)}, u32[]{:S(2)}, u32[]{:S(2)}) %collective-permute-start.1) | collective-permute-done | bytes 786464 | tf_op jit(solution)/shard_map/ppermute | solution.py:57
  337.5 33.2 %collective-permute-done.2 = bf16[384,1024]{0,1:T(8,128)(2,1)S(1)} collective-permute-done((bf16[384,1024]{0,1:T(8,128)(2,1)S(1)}, bf16[384,1024]{0,1:T(8,128)(2,1)S(1)}, u32[]{:S(2)}, u32[]{:S(2)}) %collective-permute-start.2) | collective-permute-done | bytes 786464 | tf_op jit(solution)/shard_map/ppermute | solution.py:57
  371.6 46.8 %collective-permute-done.3 = bf16[384,1024]{0,1:T(8,128)(2,1)S(1)} collective-permute-done((bf16[384,1024]{0,1:T(8,128)(2,1)S(1)}, bf16[384,1024]{0,1:T(8,128)(2,1)S(1)}, u32[]{:S(2)}, u32[]{:S(2)}) %collective-permute-start.3) | collective-permute-done | bytes 786464 | tf_op jit(solution)/shard_map/ppermute | solution.py:57
  419.3 41.5 %collective-permute-done.4 = bf16[384,1024]{0,1:T(8,128)(2,1)S(1)} collective-permute-done((bf16[384,1024]{0,1:T(8,128)(2,1)S(1)}, bf16[384,1024]{0,1:T(8,128)(2,1)S(1)}, u32[]{:S(2)}, u32[]{:S(2)}) %collective-permute-start.4) | collective-permute-done | bytes 786464 | tf_op jit(solution)/shard_map/ppermute | solution.py:57
  461.6 19.7 %collective-permute-done.5 = bf16[384,1024]{0,1:T(8,128)(2,1)S(1)} collective-permute-done((bf16[384,1024]{0,1:T(8,128)(2,1)S(1)}, bf16[384,1024]{0,1:T(8,128)(2,1)S(1)}, u32[]{:S(2)}, u32[]{:S(2)}) %collective-permute-start.5) | collective-permute-done | bytes 786464 | tf_op jit(solution)/shard_map/ppermute | solution.py:57
  482.3 19.0 %collective-permute-done.6 = bf16[384,1024]{0,1:T(8,128)(2,1)} collective-permute-done((bf16[384,1024]{0,1:T(8,128)(2,1)S(1)}, bf16[384,1024]{0,1:T(8,128)(2,1)}, u32[]{:S(2)}, u32[]{:S(2)}) %collective-permute-start.6) | collective-permute-done | bytes 786464 | tf_op jit(solution)/shard_map/ppermute | solution.py:57
  502.4 1.4 reshape_squeeze.3
  503.9 1.6 copy.25
  505.5 14.1 %collective-permute-done.7 = bf16[384,1024]{0,1:T(8,128)(2,1)} collective-permute-done((bf16[384,1024]{0,1:T(8,128)(2,1)}, bf16[384,1024]{0,1:T(8,128)(2,1)}, u32[]{:S(2)}, u32[]{:S(2)}) %collective-permute-start.7) | collective-permute-done | bytes 786464 | tf_op jit(solution)/shard_map/ppermute | solution.py:57
  523.7 1.4 constant_dynamic-update-slice_fusion.12
  531.4 6.2 %constant_dynamic-slice_fusion.2 = bf16[3072,1024]{0,1:T(8,128)(2,1)} fusion(bf16[6144,1024]{0,1:T(8,128)(2,1)S(1)} %constant_dynamic-update-slice_fusion, s32[]{:T(128)S(6)} %select_n.54), kind=kLoop, calls=%fused_computation.70 | loop fusion | bytes 12582916 | tf_op jit(solution)/shard_map/jit(_roll_dynamic)/dynamic_slice | solution.py:58
  537.7 47.5 %while.18 = (s32[]{:T(128)}, f32[8,384]{1,0:T(8,128)S(1)}, f32[8,384]{1,0:T(8,128)S(1)}, f32[384,8,128]{2,0,1:T(8,128)S(1)}, s32[]{:T(128)}, /*index=5*/bf16[307...) while((s32[]{:T(128)}, f32[8,384]{1,0:T(8,128)S(1)}, ...), condition=%wide.region_6.7_spmd.clone, body=%wide.region_1.6_spmd.clone.sunk | while | flops 823601024 | bytes 30095668 | solution.py:97
  538.5 7.3 %conditional.3 = (f32[8,384]{1,0:T(8,128)S(1)}, f32[8,384]{1,0:T(8,128)S(1)}, f32[384,8,128]{2,0,1:T(8,128)S(1)}) conditional(s32[]{:T(128)} %convert_element_type.65, (s32[]{:T(128)}, s32[512]{0:T(512)S(1)}, s32[]{:T(128)}, bf16[3072,1024]{0,1:T(8,128)(2,1)}, bf16[384,8,128]{2,0,1:T(8,128)(2,1)S(1)}, /*index=5*/f32[8,384]{1,0:T(8,128)S(1)}, ...), branch_computations={%region_2.4_spmd, %region_5.5_spmd} | conditional | flops 823601024 | bytes 30067270 | solution.py:95
  538.5 1.7 constant_dynamic-slice_fusion
  540.4 1.5 fusion.2
  542.0 2.5 bitcast_add_fusion
  546.4 7.3 %conditional.3 = (f32[8,384]{1,0:T(8,128)S(1)}, f32[8,384]{1,0:T(8,128)S(1)}, f32[384,8,128]{2,0,1:T(8,128)S(1)}) conditional(s32[]{:T(128)} %convert_element_type.65, (s32[]{:T(128)}, s32[512]{0:T(512)S(1)}, s32[]{:T(128)}, bf16[3072,1024]{0,1:T(8,128)(2,1)}, bf16[384,8,128]{2,0,1:T(8,128)(2,1)S(1)}, /*index=5*/f32[8,384]{1,0:T(8,128)S(1)}, ...), branch_computations={%region_2.4_spmd, %region_5.5_spmd} | conditional | flops 823601024 | bytes 30067270 | solution.py:95
  546.4 1.7 constant_dynamic-slice_fusion
  548.3 1.5 fusion.2
  549.8 2.5 bitcast_add_fusion
  554.3 7.3 %conditional.3 = (f32[8,384]{1,0:T(8,128)S(1)}, f32[8,384]{1,0:T(8,128)S(1)}, f32[384,8,128]{2,0,1:T(8,128)S(1)}) conditional(s32[]{:T(128)} %convert_element_type.65, (s32[]{:T(128)}, s32[512]{0:T(512)S(1)}, s32[]{:T(128)}, bf16[3072,1024]{0,1:T(8,128)(2,1)}, bf16[384,8,128]{2,0,1:T(8,128)(2,1)S(1)}, /*index=5*/f32[8,384]{1,0:T(8,128)S(1)}, ...), branch_computations={%region_2.4_spmd, %region_5.5_spmd} | conditional | flops 823601024 | bytes 30067270 | solution.py:95
  554.3 1.7 constant_dynamic-slice_fusion
  556.2 1.5 fusion.2
  557.7 2.5 bitcast_add_fusion
  562.2 7.3 %conditional.3 = (f32[8,384]{1,0:T(8,128)S(1)}, f32[8,384]{1,0:T(8,128)S(1)}, f32[384,8,128]{2,0,1:T(8,128)S(1)}) conditional(s32[]{:T(128)} %convert_element_type.65, (s32[]{:T(128)}, s32[512]{0:T(512)S(1)}, s32[]{:T(128)}, bf16[3072,1024]{0,1:T(8,128)(2,1)}, bf16[384,8,128]{2,0,1:T(8,128)(2,1)S(1)}, /*index=5*/f32[8,384]{1,0:T(8,128)S(1)}, ...), branch_computations={%region_2.4_spmd, %region_5.5_spmd} | conditional | flops 823601024 | bytes 30067270 | solution.py:95
  562.2 1.7 constant_dynamic-slice_fusion
  564.1 1.5 fusion.2
  565.6 2.5 bitcast_add_fusion
  570.0 7.3 %conditional.3 = (f32[8,384]{1,0:T(8,128)S(1)}, f32[8,384]{1,0:T(8,128)S(1)}, f32[384,8,128]{2,0,1:T(8,128)S(1)}) conditional(s32[]{:T(128)} %convert_element_type.65, (s32[]{:T(128)}, s32[512]{0:T(512)S(1)}, s32[]{:T(128)}, bf16[3072,1024]{0,1:T(8,128)(2,1)}, bf16[384,8,128]{2,0,1:T(8,128)(2,1)S(1)}, /*index=5*/f32[8,384]{1,0:T(8,128)S(1)}, ...), branch_computations={%region_2.4_spmd, %region_5.5_spmd} | conditional | flops 823601024 | bytes 30067270 | solution.py:95
  570.1 1.7 constant_dynamic-slice_fusion
  571.9 1.5 fusion.2
  573.5 2.5 bitcast_add_fusion
  577.9 7.3 %conditional.3 = (f32[8,384]{1,0:T(8,128)S(1)}, f32[8,384]{1,0:T(8,128)S(1)}, f32[384,8,128]{2,0,1:T(8,128)S(1)}) conditional(s32[]{:T(128)} %convert_element_type.65, (s32[]{:T(128)}, s32[512]{0:T(512)S(1)}, s32[]{:T(128)}, bf16[3072,1024]{0,1:T(8,128)(2,1)}, bf16[384,8,128]{2,0,1:T(8,128)(2,1)S(1)}, /*index=5*/f32[8,384]{1,0:T(8,128)S(1)}, ...), branch_computations={%region_2.4_spmd, %region_5.5_spmd} | conditional | flops 823601024 | bytes 30067270 | solution.py:95
  577.9 1.7 constant_dynamic-slice_fusion
  579.8 1.5 fusion.2
  581.3 2.5 bitcast_add_fusion
  585.8 5.7 psum.7
  (135 shorter events, 32.5 us)
Async XLA Ops:
  6.5 531.0 %all-gather.2.cloned.1.call-start = ((), (), s32[]{:S(2)}) async-start(), calls=%async_computation | async-start | bytes 7077888 | tf_op jit(solution)/shard_map/all_gather | solution.py:54
  7.7 265.0 %collective-permute-start = (bf16[3,128,1024]{2,1,0:T(8,128)(2,1)S(1)}, bf16[3,128,1024]{2,1,0:T(8,128)(2,1)}, u32[]{:S(2)}, u32[]{:S(2)}) collective-permute-start(bf16[3,128,1024]{2,1,0:T(8,128)(2,1)S(1)} %slice.21), channel_id=1, source_target_pairs={{0,4},{4,8},{8,12},{12,16},{16,20},{20,24},{24,28},{1,5},{5,9},{9,... | collective-permute-start | bytes 2359304 | tf_op jit(solution)/shard_map/ppermute | solution.py:15
  125.7 17.2 %copy-start.12 = (s32[16384]{0:T(1024)S(1)}, s32[16384]{0:T(1024)}, u32[]{:S(2)}) copy-start(s32[16384]{0:T(1024)} %constant.123) | copy-start | bytes 196612
  277.8 13.7 %slice-start.2 = ((s8[6291456]{0:T(1024)(128)(4,1)}), s8[2097152]{0:T(1024)(128)(4,1)S(1)}, s32[]{:S(2)}) async-start(s8[6291456]{0:T(1024)(128)(4,1)} %bitcast.82), calls=%async_computation.3 | async-start | bytes 4194304
  283.5 8.1 %slice-start.3 = ((s8[6291456]{0:T(1024)(128)(4,1)}), s8[4194304]{0:T(1024)(128)(4,1)S(1)}, s32[]{:S(2)}) async-start(s8[6291456]{0:T(1024)(128)(4,1)} %bitcast.82), calls=%async_computation.4 | async-start | bytes 8388608
  283.5 8.1 %copy-start.11 = (pred[128,128]{1,0:T(32,128)(4,1)S(1)}, pred[128,128]{1,0:T(32,128)(4,1)}, u32[]{:S(2)}) copy-start(pred[128,128]{1,0:T(32,128)(4,1)} %constant.120.clone) | copy-start | bytes 49156
  283.5 14.2 %slice-start = ((s8[6291456]{0:T(1024)(128)(4,1)}), s8[4194304]{0:T(1024)(128)(4,1)S(1)}, s32[]{:S(2)}) async-start(s8[6291456]{0:T(1024)(128)(4,1)} %bitcast.80), calls=%async_computation.1 | async-start | bytes 8388608
  291.6 6.1 %slice-start.1 = ((s8[6291456]{0:T(1024)(128)(4,1)}), s8[2097152]{0:T(1024)(128)(4,1)S(1)}, s32[]{:S(2)}) async-start(s8[6291456]{0:T(1024)(128)(4,1)} %bitcast.80), calls=%async_computation.2 | async-start | bytes 4194304
  291.6 6.1 %copy-start.10 = (pred[128,128]{1,0:T(32,128)(4,1)S(1)}, pred[128,128]{1,0:T(32,128)(4,1)}, u32[]{:S(2)}) copy-start(pred[128,128]{1,0:T(32,128)(4,1)} %constant.118.clone) | copy-start | bytes 49156
  308.2 28.4 %collective-permute-start.1 = (bf16[384,1024]{0,1:T(8,128)(2,1)S(1)}, bf16[384,1024]{0,1:T(8,128)(2,1)S(1)}, u32[]{:S(2)}, u32[]{:S(2)}) collective-permute-start(bf16[384,1024]{0,1:T(8,128)(2,1)S(1)} %bitcast.92), channel_id=1, source_target_pairs={{0,4},{4,8},{8,12},{12,16},{16,20},{20,24},{24,28},{28,0},{1,5},{5... | collective-permute-start | bytes 2359304 | tf_op jit(solution)/shard_map/ppermute | solution.py:57
  336.6 0.9 copy-start
  337.5 33.2 %collective-permute-start.2 = (bf16[384,1024]{0,1:T(8,128)(2,1)S(1)}, bf16[384,1024]{0,1:T(8,128)(2,1)S(1)}, u32[]{:S(2)}, u32[]{:S(2)}) collective-permute-start(bf16[384,1024]{0,1:T(8,128)(2,1)S(1)} %collective-permute-done.1), channel_id=1, source_target_pairs={{0,4},{4,8},{8,12},{12,16},{16,20},{20,24},{24,28},{28,0},{1,5},{5... | collective-permute-start | bytes 2359304 | tf_op jit(solution)/shard_map/ppermute | solution.py:57
  370.7 0.9 copy-start.2
  371.6 46.8 %collective-permute-start.3 = (bf16[384,1024]{0,1:T(8,128)(2,1)S(1)}, bf16[384,1024]{0,1:T(8,128)(2,1)S(1)}, u32[]{:S(2)}, u32[]{:S(2)}) collective-permute-start(bf16[384,1024]{0,1:T(8,128)(2,1)S(1)} %collective-permute-done.2), channel_id=1, source_target_pairs={{0,4},{4,8},{8,12},{12,16},{16,20},{20,24},{24,28},{28,0},{1,5},{5... | collective-permute-start | bytes 2359304 | tf_op jit(solution)/shard_map/ppermute | solution.py:57
  418.4 0.9 copy-start.4
  419.3 41.5 %collective-permute-start.4 = (bf16[384,1024]{0,1:T(8,128)(2,1)S(1)}, bf16[384,1024]{0,1:T(8,128)(2,1)S(1)}, u32[]{:S(2)}, u32[]{:S(2)}) collective-permute-start(bf16[384,1024]{0,1:T(8,128)(2,1)S(1)} %collective-permute-done.3), channel_id=1, source_target_pairs={{0,4},{4,8},{8,12},{12,16},{16,20},{20,24},{24,28},{28,0},{1,5},{5... | collective-permute-start | bytes 2359304 | tf_op jit(solution)/shard_map/ppermute | solution.py:57
  460.7 0.9 copy-start.6
  461.6 19.7 %collective-permute-start.5 = (bf16[384,1024]{0,1:T(8,128)(2,1)S(1)}, bf16[384,1024]{0,1:T(8,128)(2,1)S(1)}, u32[]{:S(2)}, u32[]{:S(2)}) collective-permute-start(bf16[384,1024]{0,1:T(8,128)(2,1)S(1)} %collective-permute-done.4), channel_id=1, source_target_pairs={{0,4},{4,8},{8,12},{12,16},{16,20},{20,24},{24,28},{28,0},{1,5},{5... | collective-permute-start | bytes 2359304 | tf_op jit(solution)/shard_map/ppermute | solution.py:57
  481.4 0.9 copy-start.8
  482.3 19.0 %collective-permute-start.6 = (bf16[384,1024]{0,1:T(8,128)(2,1)S(1)}, bf16[384,1024]{0,1:T(8,128)(2,1)}, u32[]{:S(2)}, u32[]{:S(2)}) collective-permute-start(bf16[384,1024]{0,1:T(8,128)(2,1)S(1)} %collective-permute-done.5), channel_id=1, source_target_pairs={{0,4},{4,8},{8,12},{12,16},{16,20},{20,24},{24,28},{28,0},{1,5},{5... | collective-permute-start | bytes 2359304 | tf_op jit(solution)/shard_map/ppermute | solution.py:57
  501.3 18.3 %collective-permute-start.7 = (bf16[384,1024]{0,1:T(8,128)(2,1)}, bf16[384,1024]{0,1:T(8,128)(2,1)}, u32[]{:S(2)}, u32[]{:S(2)}) collective-permute-start(bf16[384,1024]{0,1:T(8,128)(2,1)} %collective-permute-done.6), channel_id=1, source_target_pairs={{0,4},{4,8},{8,12},{12,16},{16,20},{20,24},{24,28},{28,0},{1,5},{5... | collective-permute-start | bytes 2359304 | tf_op jit(solution)/shard_map/ppermute | solution.py:57
  503.9 21.3 %copy-start.5 = (bf16[384,1024]{0,1:T(8,128)(2,1)S(1)}, bf16[384,1024]{0,1:T(8,128)(2,1)}, u32[]{:S(2)}) copy-start(bf16[384,1024]{0,1:T(8,128)(2,1)} %copy-done.4) | copy-start | bytes 2359300
  503.9 22.9 %copy-start.1 = (bf16[384,1024]{0,1:T(8,128)(2,1)S(1)}, bf16[384,1024]{0,1:T(8,128)(2,1)}, u32[]{:S(2)}) copy-start(bf16[384,1024]{0,1:T(8,128)(2,1)} %copy-done) | copy-start | bytes 2359300
  522.2 7.8 %copy-start.9 = (bf16[384,1024]{0,1:T(8,128)(2,1)S(1)}, bf16[384,1024]{0,1:T(8,128)(2,1)}, u32[]{:S(2)}) copy-start(bf16[384,1024]{0,1:T(8,128)(2,1)} %copy-done.8) | copy-start | bytes 2359300
  523.7 6.5 %copy-start.7 = (bf16[384,1024]{0,1:T(8,128)(2,1)S(1)}, bf16[384,1024]{0,1:T(8,128)(2,1)}, u32[]{:S(2)}) copy-start(bf16[384,1024]{0,1:T(8,128)(2,1)} %copy-done.6) | copy-start | bytes 2359300
  525.4 5.3 copy-start.3
  537.7 53.8 %copy-start.13 = (f32[1024]{0:T(1024)S(1)}, f32[1024]{0:T(1024)}, u32[]{:S(2)}) copy-start(f32[1024]{0:T(1024)} %param.15) | copy-start | bytes 12292
Sparse Core Ops, SparseCore 0:
  307.6 144.3 all-gather.1
